TPU v7x, 32 devices: a whole 2x2x4 slice. The times are simulated.
32 devices in a mesh: spot: 4 (over x, core), cell: 8 (over z, y).
Axes of the slice: x: 2, y: 2, z: 4, core: 2. Of those that a mesh axis runs over, the one named last changes fastest.
Arguments:
- logits: float32 [3, 4096, 2048], P(None, 'cell', 'spot'), may hold values from -8 to 8
- expression: float32 [3, 4096, 2048], P(None, 'cell', 'spot'), may hold values from 0.05 to 5
- measured: float32 [3, 2048, 2048], P(None, 'spot', 'cell'), may hold values from 0.05 to 5
- spot_slide: int32 [3, 2048], P(None, 'spot'), may hold values from 0 to 11, as said below
- cell_slide: int32 [3, 4096], P(None, 'cell'), may hold values from 0 to 11, as said below
- cell_valid: int32 [3, 4096], P(None, 'cell'), may hold values from 0 to 1, as said below
- gene_mask: int32 [12, 2048], replicated, may hold values from 0 to 1, as said below
Outputs:
- losses: float32 [3], replicated
- predicted: float32 [3, 2048, 2048], P(None, 'spot', 'cell')
- gene_cosine: float32 [3, 4, 2048], P(None, None, 'cell')
- spot_cosine: float32 [3, 2048], P(None, 'spot')
- logit_grad: float32 [3, 4096, 2048], P(None, 'cell', 'spot')
- expression_grad: float32 [3, 4096, 2048], P(None, 'cell', 'spot')
Inputs may be any that keep to these rules, and one draw needn't show every extreme that they name: `spot_slide`: in micro-batch b the values lie in b * 4 to (b + 1) * 4 - 1 and never fall along spots; every such slide holds 128 spots or more. `cell_slide`: in micro-batch b the values lie in b * 4 to (b + 1) * 4 - 1 and never fall along cell slots; every such slide holds 256 slots or more. `cell_valid`: the first slot of every slide is valid. `gene_mask`: every slide measures at least one gene.
All inputs are finite; a program needn't handle non-finite values.
Results may differ from a plain program's by a relative error of at most 0.0003.
Values sent between devices are 32-bit elements; how exact they have to be, the bound alone decides.
No kernel may reach another device: no remote copies, remote signals or barrier semaphores. Data moves between devices by JAX's collectives and lax.ppermute only.
A program may use at most 192 MiB of HBM per device.

v0:
```python
import jax
import jax.numpy as jnp
from jax import lax
from jax.sharding import PartitionSpec as P

highest = lax.Precision.HIGHEST
fill_value = -1e30
epsilon = 1e-06


def product(left, right):
    return jnp.dot(left, right, precision=highest, preferred_element_type=jnp.float32)


def softmax_columns(block):
    column_max = jnp.max(block, axis=0, keepdims=True)
    raised = jnp.exp(block - column_max)
    return raised / jnp.sum(raised, axis=0, keepdims=True)


def forward_columns(gathered):
    return lax.all_to_all(
        softmax_columns(gathered), "cell", split_axis=0, concat_axis=1, tiled=True
    )


def backward_columns(paired):
    mapped, grads = paired
    result = mapped * (grads - jnp.sum(mapped * grads, axis=0, keepdims=True))
    return lax.all_to_all(result, "cell", split_axis=0, concat_axis=1, tiled=True)


def per_device(logits, expression, measured, spot_slide, cell_slide, cell_valid, gene_mask):
    n_spot = lax.axis_size("spot")
    n_cell = lax.axis_size("cell")
    micro_count, cell_rows, spot_cols = logits.shape
    genes_cell = measured.shape[2]
    slides = gene_mask.shape[0] // micro_count
    cells_total = cell_rows * n_cell
    spots_total = spot_cols * n_spot
    spot_first = (lax.axis_index("spot") == 0).astype(jnp.float32)
    cell_first = (lax.axis_index("cell") == 0).astype(jnp.float32)
    gene_start = lax.axis_index("cell") * genes_cell
    gene_count = jnp.sum(gene_mask.astype(jnp.float32), axis=1)
    slide_index = jnp.arange(slides, dtype=jnp.int32)
    loss_list, pred_list, gene_list, spot_list, logit_list, expr_list = ([], [], [], [], [], [])
    for micro in range(micro_count):
        allowed = (cell_valid[micro][:, None] == 1) & (
            cell_slide[micro][:, None] == spot_slide[micro][None, :]
        )
        masked = jnp.where(allowed, logits[micro], jnp.float32(fill_value))
        layered = masked.reshape(cell_rows, n_cell, spot_cols // n_cell)
        mapping = forward_columns(
            lax.all_to_all(layered, "cell", split_axis=1, concat_axis=0, tiled=True)
        ).reshape(cell_rows, spot_cols)
        expression_full = lax.all_gather(expression[micro], "spot", axis=1, tiled=True)
        predicted = lax.psum_scatter(
            product(mapping.T, expression_full), "cell", scatter_dimension=1, tiled=True
        )
        true_block = measured[micro]
        onehot = ((spot_slide[micro] - micro * slides)[None, :] == slide_index[:, None]).astype(
            jnp.float32
        )
        pred_sq, pred_true, true_sq = lax.psum(
            (
                product(onehot, predicted * predicted),
                product(onehot, predicted * true_block),
                product(onehot, true_block * true_block),
            ),
            "spot",
        )
        gene_scale = lax.rsqrt(pred_sq * true_sq + epsilon)
        gene_cos = pred_true * gene_scale
        slide_mask = gene_mask[micro * slides : (micro + 1) * slides].astype(jnp.float32)
        local_mask = lax.dynamic_slice_in_dim(slide_mask, gene_start, genes_cell, 1)
        weight = local_mask / (slides * gene_count[micro * slides : (micro + 1) * slides][:, None])
        gene_part = jnp.sum(weight * gene_cos) * spot_first
        spot_mask = product(onehot.T, local_mask)
        spot_pp, spot_pt, spot_tt = lax.psum(
            (
                jnp.sum(spot_mask * predicted * predicted, axis=1),
                jnp.sum(spot_mask * predicted * true_block, axis=1),
                jnp.sum(spot_mask * true_block * true_block, axis=1),
            ),
            "cell",
        )
        spot_scale = lax.rsqrt(spot_pp * spot_tt + epsilon)
        spot_cos = spot_pt * spot_scale
        spot_part = jnp.sum(spot_cos) / spots_total * cell_first
        loss_list.append(-(gene_part + spot_part))
        first_coef = product(onehot.T, weight * gene_scale)
        second_coef = product(onehot.T, weight * pred_true * true_sq * gene_scale**3)
        gene_grad = first_coef * true_block - second_coef * predicted
        spot_grad = (
            spot_mask
            * (
                true_block * spot_scale[:, None]
                - (spot_pt * spot_tt * spot_scale**3)[:, None] * predicted
            )
            / spots_total
        )
        pred_grad = -cells_total * (gene_grad + spot_grad)
        shard_cols = lax.all_gather(pred_grad, "cell", axis=1, tiled=True)
        summed = product(expression_full, shard_cols.T)
        placed = product(mapping, shard_cols)
        expr_list.append(lax.psum_scatter(placed, "spot", scatter_dimension=1, tiled=True))
        shaped = (cell_rows, n_cell, spot_cols // n_cell)
        logit_block = backward_columns(
            (
                lax.all_to_all(
                    mapping.reshape(shaped), "cell", split_axis=1, concat_axis=0, tiled=True
                ),
                lax.all_to_all(
                    summed.reshape(shaped), "cell", split_axis=1, concat_axis=0, tiled=True
                ),
            )
        ).reshape(cell_rows, spot_cols)
        logit_list.append(logit_block)
        pred_list.append(predicted)
        gene_list.append(gene_cos)
        spot_list.append(spot_cos)
    losses = lax.psum(jnp.stack(loss_list), ("spot", "cell"))
    return (
        losses,
        jnp.stack(pred_list),
        jnp.stack(gene_list),
        jnp.stack(spot_list),
        jnp.stack(logit_list),
        jnp.stack(expr_list),
    )


def solution(mesh):
    return jax.shard_map(
        per_device,
        mesh=mesh,
        in_specs=(
            P(None, "cell", "spot"),
            P(None, "cell", "spot"),
            P(None, "spot", "cell"),
            P(None, "spot"),
            P(None, "cell"),
            P(None, "cell"),
            P(),
        ),
        out_specs=(
            P(),
            P(None, "spot", "cell"),
            P(None, None, "cell"),
            P(None, "spot"),
            P(None, "cell", "spot"),
            P(None, "cell", "spot"),
        ),
        check_vma=False,
    )
```

profile of v0, /device:TPU:0, one launch (start us, length us, event | category | flops | bytes accessed | tf_op | source)
XLA Modules:
  0.0 1044.3 jit_solution(4495634205946192081)
XLA Ops:
  16.8 32.9 %all_to_all.261 = f32[512,8,64]{0,2,1:T(8,128)S(1)} all-to-all(f32[512,8,64]{0,2,1:T(8,128)S(1)} %and_select_fusion.1), channel_id=1, replica_groups=mesh['spot'=4,'cell'=8] {'cell'}, dimensions={1} | all-to-all | bytes 2097152 | tf_op jit(solution)/shard_map/all_to_all | solution.py:54
  53.7 29.1 %all_to_all.262 = f32[8,1,32768]{2,1,0:T(1,128)S(1)} all-to-all(f32[8,1,32768]{2,1,0:T(1,128)S(1)} %reshape.525), channel_id=1, replica_groups=mesh['spot'=4,'cell'=8] {'cell'}, dimensions={0} | all-to-all | bytes 2097152 | tf_op jit(solution)/shard_map/all_to_all | solution.py:22
  92.3 10.3 fusion.6
  104.4 28.4 %all_to_all.263 = f32[512,8,64]{0,2,1:T(8,128)S(1)} all-to-all(f32[512,8,64]{0,2,1:T(8,128)S(1)} %and_select_fusion), channel_id=1, replica_groups=mesh['spot'=4,'cell'=8] {'cell'}, dimensions={1} | all-to-all | bytes 2097152 | tf_op jit(solution)/shard_map/all_to_all | solution.py:54
  139.4 50.7 %all_to_all.264 = f32[8,1,32768]{2,1,0:T(1,128)S(1)} all-to-all(f32[8,1,32768]{2,1,0:T(1,128)} %reshape.521), channel_id=1, replica_groups=mesh['spot'=4,'cell'=8] {'cell'}, dimensions={0} | all-to-all | bytes 2097152 | tf_op jit(solution)/shard_map/all_to_all | solution.py:22
  190.1 4.5 reduce.43
  203.1 10.3 fusion.2
  215.3 40.7 %all_to_all.265 = f32[512,8,64]{0,2,1:T(8,128)S(1)} all-to-all(f32[512,8,64]{0,2,1:T(8,128)S(1)} %and_select_fusion.2), channel_id=1, replica_groups=mesh['spot'=4,'cell'=8] {'cell'}, dimensions={1} | all-to-all | bytes 2097152 | tf_op jit(solution)/shard_map/all_to_all | solution.py:54
  262.5 54.7 %all_to_all.266 = f32[8,1,32768]{2,1,0:T(1,128)S(1)} all-to-all(f32[8,1,32768]{2,1,0:T(1,128)} %reshape.523), channel_id=1, replica_groups=mesh['spot'=4,'cell'=8] {'cell'}, dimensions={0} | all-to-all | bytes 2097152 | tf_op jit(solution)/shard_map/all_to_all | solution.py:22
  317.2 4.5 reduce.47
  330.1 10.4 fusion.10
  346.4 19.0 %reduce-scatter.11.cloned.1.call-done = f32[512,256]{1,0:T(8,128)} async-done(((f32[512,2048]{1,0:T(8,128)}), f32[512,256]{1,0:T(8,128)}) %reduce-scatter.11.cloned.1.call-update) | async-done | bytes 524304 | tf_op jit(solution)/shard_map/reduce_scatter | solution.py:57
  369.4 87.8 %reduce-scatter.7.cloned.1.call-done = f32[512,256]{1,0:T(8,128)} async-done(((f32[512,2048]{1,0:T(8,128)}), f32[512,256]{1,0:T(8,128)}) %reduce-scatter.7.cloned.1.call-update) | async-done | bytes 524304 | tf_op jit(solution)/shard_map/reduce_scatter | solution.py:57
  459.9 11.0 %all-reduce.1 = (f32[4,256]{1,0:T(4,128)S(1)}, f32[4,256]{1,0:T(4,128)S(1)}, f32[4,256]{1,0:T(4,128)S(1)}, f32[4,256]{1,0:T(4,128)S(1)}, f32[4,256]{1,0:T(4,128)...) all-reduce(f32[4,256]{1,0:T(4,128)S(1)} %fusion.33, ...), channel_id=1, replica_groups=mesh['spot'=4,'cell'=8] {'spot'}, use_global_device_ids=true, to_apply=%region_32.33 | all-reduce | flops 9216 | bytes 73728 | tf_op jit(solution)/shard_map/psum | solution.py:64
  475.5 36.4 %all-reduce = (f32[512]{0:T(512)S(1)}, f32[512]{0:T(512)S(1)}, f32[512]{0:T(512)S(1)}, f32[512]{0:T(512)S(1)}, f32[512]{0:T(512)S(1)}, /*index=5*/f32[512]{0:T(5...) all-reduce(f32[512]{0:T(512)S(1)} %get-tuple-element.32, ...), channel_id=1, replica_groups=mesh['spot'=4,'cell'=8] {'cell'}, use_global_device_ids=true, to_apply=%region_37.38 | all-reduce | flops 4608 | bytes 36864 | tf_op jit(solution)/shard_map/psum | solution.py:79
  520.8 65.0 %all-gather.14.cloned.1.call-done = f32[512,2048]{1,0:T(8,128)} async-done(((f32[512,256]{1,0:T(8,128)}), f32[512,2048]{1,0:T(8,128)}) %all-gather.14.cloned.1.call-update) | async-done | bytes 4194320 | tf_op jit(solution)/shard_map/all_gather | solution.py:103
  585.8 10.2 fusion.123
  596.5 64.8 %all-gather.12.cloned.1.call-done = f32[512,2048]{1,0:T(8,128)} async-done(((f32[512,256]{1,0:T(8,128)}), f32[512,2048]{1,0:T(8,128)}) %all-gather.12.cloned.1.call-update) | async-done | bytes 4194320 | tf_op jit(solution)/shard_map/all_gather | solution.py:103
  661.3 9.9 fusion.122
  679.7 34.9 %all-to-all-done.6 = f32[512,8,64]{0,2,1:T(8,128)S(1)} async-done(((f32[512,8,64]{0,2,1:T(8,128)}), f32[512,8,64]{0,2,1:T(8,128)S(1)}, u32[]{:S(2)}, u32[]{:S(2)}) %all-to-all-start.6) | async-done | bytes 1048608 | tf_op jit(solution)/shard_map/all_to_all | solution.py:110
  720.5 47.9 %all-to-all-done.9 = f32[512,8,64]{0,2,1:T(8,128)} async-done(((f32[512,8,64]{0,2,1:T(8,128)}), f32[512,8,64]{0,2,1:T(8,128)}, u32[]{:S(2)}, u32[]{:S(2)}) %all-to-all-start.9) | async-done | bytes 1048608 | tf_op jit(solution)/shard_map/all_to_all | solution.py:110
  775.9 10.3 fusion.8
  786.1 12.0 %all-to-all-done.12 = f32[512,8,64]{0,2,1:T(8,128)S(1)} async-done(((f32[512,8,64]{0,2,1:T(8,128)}), f32[512,8,64]{0,2,1:T(8,128)S(1)}, u32[]{:S(2)}, u32[]{:S(2)}) %all-to-all-start.12) | async-done | bytes 1048608 | tf_op jit(solution)/shard_map/all_to_all | solution.py:110
  801.9 10.3 fusion
  812.2 15.1 %all-to-all-done.7 = f32[512,8,64]{0,2,1:T(8,128)S(1)} async-done(((f32[512,8,64]{0,2,1:T(8,128)}), f32[512,8,64]{0,2,1:T(8,128)S(1)}, u32[]{:S(2)}, u32[]{:S(2)}) %all-to-all-start.7) | async-done | bytes 1048608 | tf_op jit(solution)/shard_map/all_to_all | solution.py:113
  831.6 10.5 %fusion.121 = f32[512,2048]{1,0:T(8,128)} fusion(f32[512,512]{0,1:T(8,128)S(1)} %bitcast.231, f32[512,2048]{1,0:T(8,128)} %all-gather.10.cloned.1.call-done), kind=kOutput, calls=%fused_computation.193 | convolution fusion | flops 6442450944 | bytes 9437184 | tf_op jit(solution)/shard_map/dot_general | solution.py:12
  842.1 10.6 %fusion.4 = f32[512,512]{1,0:T(8,128)} fusion(f32[512,2048]{1,0:T(8,128)} %all-gather.12.cloned.1.call-done, f32[1,512,2048]{2,1,0:T(8,128)} %all-gather.18.cloned.1.call-done), kind=kOutput, calls=%fused_computation.4 | convolution fusion | flops 6442450944 | bytes 9437184 | tf_op jit(solution)/shard_map/dot_general | solution.py:12
  857.0 4.7 all-to-all-start.10
  872.9 14.1 %all-to-all-done.10 = f32[512,8,64]{0,2,1:T(8,128)} async-done(((f32[512,8,64]{0,2,1:T(8,128)}), f32[512,8,64]{0,2,1:T(8,128)}, u32[]{:S(2)}, u32[]{:S(2)}) %all-to-all-start.10) | async-done | bytes 1048608 | tf_op jit(solution)/shard_map/all_to_all | solution.py:113
  904.2 12.4 %all-to-all-done.14 = f32[8,1,32768]{2,1,0:T(1,128)} async-done(((f32[8,1,32768]{2,1,0:T(1,128)}), f32[8,1,32768]{2,1,0:T(1,128)}, u32[]{:S(2)}, u32[]{:S(2)}) %all-to-all-start.14) | async-done | bytes 1048608 | tf_op jit(solution)/shard_map/all_to_all | solution.py:30
  925.0 21.3 %all-to-all-done.11 = f32[8,1,32768]{2,1,0:T(1,128)} async-done(((f32[8,1,32768]{2,1,0:T(1,128)}), f32[8,1,32768]{2,1,0:T(1,128)}, u32[]{:S(2)}, u32[]{:S(2)}) %all-to-all-start.11) | async-done | bytes 1048608 | tf_op jit(solution)/shard_map/all_to_all | solution.py:30
  957.2 41.1 %psum.151 = f32[3]{0:T(128)} all-reduce(f32[3]{0:T(128)S(1)} %pad_maximum_fusion.5), channel_id=1, replica_groups=mesh['spot'=4,'cell'=8] {'spot','cell'}, use_global_device_ids=true, to_apply=%region_43.44 | all-reduce | flops 3 | bytes 24 | tf_op jit(solution)/shard_map/psum | solution.py:122
  (195 shorter events, 199.6 us)
Async XLA Ops:
  7.2 85.1 %all-gather.18.cloned.1.call-start = ((), (), s32[]{:S(2)}) async-start(), calls=%async_computation.31 | async-start | bytes 5242880 | tf_op jit(solution)/shard_map/all_gather | solution.py:56
  10.9 192.2 %all-gather.20.cloned.1.call-start = ((), (), s32[]{:S(2)}) async-start(), calls=%async_computation.32 | async-start | bytes 5242880 | tf_op jit(solution)/shard_map/all_gather | solution.py:56
  11.6 318.5 %all-gather.16.cloned.1.call-start = ((), (), s32[]{:S(2)}) async-start(), calls=%async_computation.30 | async-start | bytes 5242880 | tf_op jit(solution)/shard_map/all_gather | solution.py:56
  12.3 332.7 %reduce-scatter.9.cloned.1.call-start = ((), (), s32[]{:S(2)}) async-start(), calls=%async_computation.22 | async-start | bytes 4718592 | tf_op jit(solution)/shard_map/reduce_scatter | solution.py:57
  12.5 4.0 copy-start.15
  88.6 14.0 %copy-start.1 = (f32[4096,1,64]{2,1,0:T(1,128)}, f32[4096,1,64]{2,1,0:T(1,128)S(1)}, u32[]{:S(2)}) copy-start(f32[4096,1,64]{2,1,0:T(1,128)S(1)} %reshape.526) | copy-start | bytes 3145732
  102.6 262.9 %reduce-scatter.11.cloned.1.call-start = ((), (), s32[]{:S(2)}) async-start(), calls=%async_computation.23 | async-start | bytes 4718592 | tf_op jit(solution)/shard_map/reduce_scatter | solution.py:57
  198.4 15.0 %copy-start.3 = (f32[4096,1,64]{2,1,0:T(1,128)}, f32[4096,1,64]{2,1,0:T(1,128)S(1)}, u32[]{:S(2)}) copy-start(f32[4096,1,64]{2,1,0:T(1,128)S(1)} %reshape.522) | copy-start | bytes 3145732
  213.4 243.8 %reduce-scatter.7.cloned.1.call-start = ((), (), s32[]{:S(2)}) async-start(), calls=%async_computation.21 | async-start | bytes 4718592 | tf_op jit(solution)/shard_map/reduce_scatter | solution.py:57
  325.5 4.6 copy-start.5
  340.6 245.3 %all-gather.14.cloned.1.call-start = ((), (), s32[]{:S(2)}) async-start(), calls=%async_computation.26 | async-start | bytes 4718592 | tf_op jit(solution)/shard_map/all_gather | solution.py:103
  345.0 127.1 %copy-start.9 = (f32[512,256]{1,0:T(8,128)S(1)}, f32[512,256]{1,0:T(8,128)}, u32[]{:S(2)}) copy-start(f32[512,256]{1,0:T(8,128)} %reduce-scatter.9.cloned.1.call-done) | copy-start | bytes 1572868
  514.7 146.6 %all-gather.12.cloned.1.call-start = ((), (), s32[]{:S(2)}) async-start(), calls=%async_computation.25 | async-start | bytes 4718592 | tf_op jit(solution)/shard_map/all_gather | solution.py:103
  517.6 258.3 %all-gather.10.cloned.1.call-start = ((), (), s32[]{:S(2)}) async-start(), calls=%async_computation.24 | async-start | bytes 4718592 | tf_op jit(solution)/shard_map/all_gather | solution.py:103
  520.8 512.7 %reduce-scatter.17.cloned.1.call-start = ((), (), s32[]{:S(2)}) async-start(), calls=%async_computation.29 | async-start | bytes 5242880 | tf_op jit(solution)/shard_map/reduce_scatter | solution.py:106
  596.0 437.4 %reduce-scatter.15.cloned.1.call-start = ((), (), s32[]{:S(2)}) async-start(), calls=%async_computation.28 | async-start | bytes 5242880 | tf_op jit(solution)/shard_map/reduce_scatter | solution.py:106
  671.3 6.9 copy-start.2
  674.6 40.1 %all-to-all-start.6 = ((f32[512,8,64]{0,2,1:T(8,128)}), f32[512,8,64]{0,2,1:T(8,128)S(1)}, u32[]{:S(2)}, u32[]{:S(2)}) async-start(f32[512,8,64]{0,2,1:T(8,128)} %copy.90), calls=%async_computation.9 | async-start | bytes 2097152 | tf_op jit(solution)/shard_map/all_to_all | solution.py:110
  679.7 39.2 %copy-start.4 = (f32[4096,1,64]{2,1,0:T(1,128)S(1)}, f32[4096,1,64]{2,1,0:T(1,128)}, u32[]{:S(2)}) copy-start(f32[4096,1,64]{2,1,0:T(1,128)} %copy-done.3) | copy-start | bytes 3145732
  714.6 53.7 %all-to-all-start.9 = ((f32[512,8,64]{0,2,1:T(8,128)}), f32[512,8,64]{0,2,1:T(8,128)}, u32[]{:S(2)}, u32[]{:S(2)}) async-start(f32[512,8,64]{0,2,1:T(8,128)} %copy.97), calls=%async_computation.12 | async-start | bytes 2097152 | tf_op jit(solution)/shard_map/all_to_all | solution.py:110
  768.3 29.8 %all-to-all-start.12 = ((f32[512,8,64]{0,2,1:T(8,128)}), f32[512,8,64]{0,2,1:T(8,128)S(1)}, u32[]{:S(2)}, u32[]{:S(2)}) async-start(f32[512,8,64]{0,2,1:T(8,128)} %copy.104), calls=%async_computation.15 | async-start | bytes 2097152 | tf_op jit(solution)/shard_map/all_to_all | solution.py:110
  798.1 29.2 %all-to-all-start.7 = ((f32[512,8,64]{0,2,1:T(8,128)}), f32[512,8,64]{0,2,1:T(8,128)S(1)}, u32[]{:S(2)}, u32[]{:S(2)}) async-start(f32[512,8,64]{0,2,1:T(8,128)} %bitcast.245), calls=%async_computation.10 | async-start | bytes 2097152 | tf_op jit(solution)/shard_map/all_to_all | solution.py:113
  812.2 19.4 %copy-start.6 = (f32[512,8,1,64]{0,3,1,2:T(8,128)S(1)}, f32[512,8,1,64]{0,3,1,2:T(8,128)}, u32[]{:S(2)}) copy-start(f32[512,8,1,64]{0,3,1,2:T(8,128)} %copy.73) | copy-start | bytes 3145732
  827.3 29.7 %all-to-all-start.13 = ((f32[512,8,64]{0,2,1:T(8,128)}), f32[512,8,64]{0,2,1:T(8,128)}, u32[]{:S(2)}, u32[]{:S(2)}) async-start(f32[512,8,64]{0,2,1:T(8,128)} %bitcast.243), calls=%async_computation.16 | async-start | bytes 2097152 | tf_op jit(solution)/shard_map/all_to_all | solution.py:113
  831.6 201.9 %reduce-scatter.13.cloned.1.call-start = ((), (), s32[]{:S(2)}) async-start(), calls=%async_computation.27 | async-start | bytes 5242880 | tf_op jit(solution)/shard_map/reduce_scatter | solution.py:106
  842.1 19.5 %copy-start.8 = (f32[512,8,64]{0,2,1:T(8,128)S(1)}, f32[512,8,64]{0,2,1:T(8,128)}, u32[]{:S(2)}) copy-start(f32[512,8,64]{0,2,1:T(8,128)} %copy-done.7) | copy-start | bytes 3145732
  857.0 30.0 %all-to-all-start.10 = ((f32[512,8,64]{0,2,1:T(8,128)}), f32[512,8,64]{0,2,1:T(8,128)}, u32[]{:S(2)}, u32[]{:S(2)}) async-start(f32[512,8,64]{0,2,1:T(8,128)} %bitcast.244), calls=%async_computation.13 | async-start | bytes 2097152 | tf_op jit(solution)/shard_map/all_to_all | solution.py:113
  887.0 29.7 %all-to-all-start.14 = ((f32[8,1,32768]{2,1,0:T(1,128)}), f32[8,1,32768]{2,1,0:T(1,128)}, u32[]{:S(2)}, u32[]{:S(2)}) async-start(f32[8,1,32768]{2,1,0:T(1,128)} %reshape.527), calls=%async_computation.17 | async-start | bytes 2097152 | tf_op jit(solution)/shard_map/all_to_all | solution.py:30
  916.7 29.6 %all-to-all-start.11 = ((f32[8,1,32768]{2,1,0:T(1,128)}), f32[8,1,32768]{2,1,0:T(1,128)}, u32[]{:S(2)}, u32[]{:S(2)}) async-start(f32[8,1,32768]{2,1,0:T(1,128)} %reshape.529), calls=%async_computation.14 | async-start | bytes 2097152 | tf_op jit(solution)/shard_map/all_to_all | solution.py:30
  922.9 76.6 %copy-start.10 = (f32[512,256]{1,0:T(8,128)S(1)}, f32[512,256]{1,0:T(8,128)}, u32[]{:S(2)}) copy-start(f32[512,256]{1,0:T(8,128)} %reduce-scatter.9.cloned.1.call-done) | copy-start | bytes 1572868
  922.9 76.6 %copy-start.11 = (f32[512,256]{1,0:T(8,128)S(1)}, f32[512,256]{1,0:T(8,128)}, u32[]{:S(2)}) copy-start(f32[512,256]{1,0:T(8,128)} %reduce-scatter.11.cloned.1.call-done) | copy-start | bytes 1572868
  946.3 74.5 %all-to-all-start.8 = ((f32[8,1,32768]{2,1,0:T(1,128)}), f32[8,1,32768]{2,1,0:T(1,128)}, u32[]{:S(2)}, u32[]{:S(2)}) async-start(f32[8,1,32768]{2,1,0:T(1,128)} %reshape.531), calls=%async_computation.11 | async-start | bytes 2097152 | tf_op jit(solution)/shard_map/all_to_all | solution.py:30
  (7 other events, 16.4 us)
Sparse Core Ops, SparseCore 0:
  11.0 37.1 all-gather.17
  49.8 34.4 all-gather.19
  85.8 34.4 all-gather.15
  123.8 124.5 reduce-scatter.8
  251.8 113.5 reduce-scatter.10
  368.9 88.2 reduce-scatter.6
  514.8 71.0 all-gather.13
  588.5 72.8 all-gather.11
  663.4 112.4 all-gather.9
  778.2 43.0 reduce-scatter.16
  823.9 44.4 reduce-scatter.14
  870.7 44.4 reduce-scatter.12
where the time goes:
time: 1050 us; the launch traced here: 1040 us
  waiting for transfers between devices  404 us (38%)
  blocking collectives  325 us (31%)
  matrix products  117 us (11%)
  local copies, waits for them, and re-layouts  85.8 us (8%)
  other arithmetic  55.1 us (5%)
  starting transfers between devices  38.2 us (4%)
  between operations  18.9 us (2%)
    all_to_all x3, blocking collectives, forward_columns(): lax.all_to_all(softmax_columns(gathered), 'cell', split_axis=0, concat_ax...  135 us
    all_gather x3, waiting for transfers between devices, per_device(): shard_cols = lax.all_gather(pred_grad, 'cell', axis=1, tiled=True)  134 us
    dot_general x27, matrix products, product(): jnp.dot(left, right, precision=highest, preferred_element_type=jnp.float32)  117 us
    reduce_scatter x3, waiting for transfers between devices, per_device(): lax.psum_scatter(product(mapping.T, expression_full), 'cell', scatter_dim...  107 us
    all_to_all x3, blocking collectives, per_device(): lax.all_to_all(layered, 'cell', split_axis=1, concat_axis=0, tiled=True)  102 us
    all_to_all x3, waiting for transfers between devices, per_device(): lax.all_to_all(mapping.reshape(shaped), 'cell', split_axis=1, concat_axis...  94.8 us
    unnamed x58, local copies, waits for them, and re-layouts  47.6 us
    psum x1, blocking collectives, per_device(): losses = lax.psum(jnp.stack(loss_list), ('spot', 'cell'))  41.1 us
  transfers between devices with their start and end apart: 21, of which 13 were waited for; matrix products, arithmetic and copies ran while one was open for 23% of the time, Pallas kernels for 0%

commit v1 on v0

v1 whole, which is shorter than its diff:
```python
import jax
import jax.numpy as jnp
from jax import lax
from jax.sharding import PartitionSpec as P

epsilon = 1e-06


def dot(left, right, dims):
    return lax.dot_general(
        left,
        right,
        (dims, ((), ())),
        precision=lax.Precision.HIGH,
        preferred_element_type=jnp.float32,
    )


def small_dot(left, right):
    return jnp.dot(
        left, right, precision=lax.Precision.HIGHEST, preferred_element_type=jnp.float32
    )


def cycle(count):
    wide = 1
    while 2 * (wide * 2) ** 2 <= count and count % (wide * 2) == 0:
        wide *= 2
    deep = count // wide
    if wide == 1 or deep % 2:
        return list(range(count))
    walk = []
    for row in range(deep):
        columns = range(1, wide)
        walk += [row * wide + c for c in (columns if row % 2 == 0 else reversed(columns))]
    return walk + [row * wide for row in reversed(range(deep))]


def per_device(logits, expression, measured, spot_slide, cell_slide, cell_valid, gene_mask):
    n_spot = lax.axis_size("spot")
    n_cell = lax.axis_size("cell")
    micro_count, cell_rows, spot_cols = logits.shape
    genes_cell = measured.shape[2]
    ratio = expression.shape[2] // genes_cell
    slides = gene_mask.shape[0] // micro_count
    cells_total = cell_rows * n_cell
    spots_total = spot_cols * n_spot
    spot_first = (lax.axis_index("spot") == 0).astype(jnp.float32)
    cell_first = (lax.axis_index("cell") == 0).astype(jnp.float32)
    cell_here = lax.axis_index("cell")
    gene_start = cell_here * genes_cell
    ring = cycle(n_cell)
    place = [ring.index(c) for c in range(n_cell)]
    here = jnp.asarray(place, jnp.int32)[cell_here]
    ring_table = jnp.asarray(ring, jnp.int32)
    half = n_cell // 2
    rows_half = spot_cols // 2
    forth = [(ring[q], ring[(q + 1) % n_cell]) for q in range(n_cell)]
    back = [(b, a) for a, b in forth]

    def owner(step):
        return ring_table[(here + step) % n_cell]

    def right(value):
        return lax.ppermute(value, "cell", forth)

    def left(value):
        return lax.ppermute(value, "cell", back)

    def gene_block(full, index):
        start = (index // ratio, 0, (index % ratio) * genes_cell)
        return lax.dynamic_slice(full, start, (1, cell_rows, genes_cell))[0]

    gene_count = jnp.sum(gene_mask.astype(jnp.float32), axis=1)
    slide_index = jnp.arange(slides, dtype=jnp.int32)
    allowed = (cell_valid[:, :, None] == 1) & (cell_slide[:, :, None] == spot_slide[:, None, :])
    raised = jnp.where(allowed, jnp.exp(logits), 0.0)
    inverse = 1.0 / lax.psum(jnp.sum(raised, axis=1), "cell")

    loss_list, pred_list, gene_list, spot_list, logit_list, expr_list = ([], [], [], [], [], [])
    for micro in range(micro_count):
        weights = raised[micro]
        full = lax.all_gather(expression[micro], "spot")

        def part(step):
            return dot(weights, gene_block(full, owner(step)), ((0,), (0,)))

        first = part(half)
        a = right(first[:rows_half])
        b = left(first[rows_half:])
        for k in range(half - 1, 0, -1):
            pr, pl = part(k), part(-k)
            if k == half - 1:
                pr = jnp.concatenate([pr[:rows_half] + a, pr[rows_half:]])
                pl = jnp.concatenate([pl[:rows_half], pl[rows_half:] + b])
            else:
                pr, pl = pr + a, pl + b
            a, b = right(pr), left(pl)
        own = part(0)
        predicted = (own + a + b) * inverse[micro][:, None]
        true_block = measured[micro]
        onehot = ((spot_slide[micro] - micro * slides)[None, :] == slide_index[:, None]).astype(
            jnp.float32
        )
        pred_sq, pred_true, true_sq = lax.psum(
            (
                small_dot(onehot, predicted * predicted),
                small_dot(onehot, predicted * true_block),
                small_dot(onehot, true_block * true_block),
            ),
            "spot",
        )
        gene_scale = lax.rsqrt(pred_sq * true_sq + epsilon)
        gene_cos = pred_true * gene_scale
        slide_mask = gene_mask[micro * slides : (micro + 1) * slides].astype(jnp.float32)
        local_mask = lax.dynamic_slice_in_dim(slide_mask, gene_start, genes_cell, 1)
        weight = local_mask / (slides * gene_count[micro * slides : (micro + 1) * slides][:, None])
        gene_part = jnp.sum(weight * gene_cos) * spot_first
        spot_mask = small_dot(onehot.T, local_mask)
        first_coef = small_dot(onehot.T, weight * gene_scale)
        second_coef = small_dot(onehot.T, weight * pred_true * true_sq * gene_scale**3)
        gene_grad = first_coef * true_block - second_coef * predicted
        spot_pp, spot_pt, spot_tt, gene_dot = lax.psum(
            (
                jnp.sum(spot_mask * predicted * predicted, axis=1),
                jnp.sum(spot_mask * predicted * true_block, axis=1),
                jnp.sum(spot_mask * true_block * true_block, axis=1),
                jnp.sum(gene_grad * predicted, axis=1),
            ),
            "cell",
        )
        spot_scale = lax.rsqrt(spot_pp * spot_tt + epsilon)
        spot_cos = spot_pt * spot_scale
        spot_part = jnp.sum(spot_cos) / spots_total * cell_first
        loss_list.append(-(gene_part + spot_part))
        spot_coef = spot_pt * spot_tt * spot_scale**3
        spot_grad = (
            spot_mask
            * (true_block * spot_scale[:, None] - spot_coef[:, None] * predicted)
            / spots_total
        )
        pred_grad = -cells_total * (gene_grad + spot_grad)
        centre = -cells_total * (
            gene_dot + (spot_pt * spot_scale - spot_coef * spot_pp) / spots_total
        )
        mapping = weights * inverse[micro][None, :]

        blocks = [(0, pred_grad)]
        a = b = pred_grad
        for k in range(1, half):
            a, b = right(a), left(b)
            blocks += [(-k, a), (k, b)]
        a, b = right(a[:rows_half]), left(b[rows_half:])
        blocks.append((half, jnp.concatenate([a, b])))
        mapping_grad = 0.0
        placed = jnp.zeros((n_spot, cell_rows, expression.shape[2]), jnp.float32)
        for step, block in blocks:
            index = owner(step)
            mapping_grad = mapping_grad + dot(gene_block(full, index), block, ((1,), (1,)))
            placed = lax.dynamic_update_slice(
                placed,
                dot(mapping, block, ((1,), (0,)))[None],
                (index // ratio, 0, (index % ratio) * genes_cell),
            )
        expr_list.append(lax.psum_scatter(placed, "spot", scatter_dimension=0))
        logit_list.append(mapping * (mapping_grad - centre[None, :]))
        pred_list.append(predicted)
        gene_list.append(gene_cos)
        spot_list.append(spot_cos)
    losses = lax.psum(jnp.stack(loss_list), ("spot", "cell"))
    return (
        losses,
        jnp.stack(pred_list),
        jnp.stack(gene_list),
        jnp.stack(spot_list),
        jnp.stack(logit_list),
        jnp.stack(expr_list),
    )


def solution(mesh):
    return jax.shard_map(
        per_device,
        mesh=mesh,
        in_specs=(
            P(None, "cell", "spot"),
            P(None, "cell", "spot"),
            P(None, "spot", "cell"),
            P(None, "spot"),
            P(None, "cell"),
            P(None, "cell"),
            P(),
        ),
        out_specs=(
            P(),
            P(None, "spot", "cell"),
            P(None, None, "cell"),
            P(None, "spot"),
            P(None, "cell", "spot"),
            P(None, "cell", "spot"),
        ),
        check_vma=False,
    )
```

time: 1050 us -> 545 us (0.52)
  waiting for transfers between devices: 404 us -> 181 us
  blocking collectives: 325 us -> 111 us
  local copies, waits for them, and re-layouts: 85.8 us -> 24.5 us
  other arithmetic: 55.1 us -> 25.7 us
  between operations: 18.9 us -> 47.5 us
  matrix products: 117 us -> 92.7 us
  starting transfers between devices: 38.2 us -> 57.5 us
    all_to_all x6 -> x0, blocking collectives: 237 us -> none  [the longest x3 135 us: forward_columns(): lax.all_to_all(softmax_columns(gathered), 'cell', split_axis=0, concat_ax...]
    all_to_all x9 -> x0, waiting for transfers between devices: 162 us -> none  [the longest x3 94.8 us: per_device(): lax.all_to_all(mapping.reshape(shaped), 'cell', split_axis=1, concat_axis...]
    ppermute x0 -> x48, waiting for transfers between devices: none -> 142 us  [the longest x24 85.6 us: right(): return lax.ppermute(value, 'cell', forth)]
    reduce_scatter x6 -> x3, waiting for transfers between devices: 107 us -> 0.01 us  [per_device(): expr_list.append(lax.psum_scatter(placed, 'spot', scatter_dimension=0))]
    all_gather x6 -> x3, waiting for transfers between devices: 134 us -> 37.6 us  [per_device(): full = lax.all_gather(expression[micro], 'spot')]
    ppermute x0 -> x48, starting transfers between devices: none -> 57 us  [the longest x24 34.5 us: left(): return lax.ppermute(value, 'cell', back)]
    unnamed x58 -> x149, local copies, waits for them, and re-layouts: 47.6 us -> 9.81 us
    all_to_all x9 -> x0, starting transfers between devices: 37.1 us -> none  [the longest x3 12.8 us: backward_columns(): lax.all_to_all(result, 'cell', split_axis=0, concat_axis=1, tiled=True)]
  transfers between devices with their start and end apart: 21 -> 54, of which waited for: 13 -> 38; matrix products, arithmetic and copies ran while one was open for 23% -> 22% of each run, Pallas kernels for 0% -> 0%
where the time goes in v1:
time: 545 us; the launch traced here: 539 us
  waiting for transfers between devices  181 us (33%)
  blocking collectives  111 us (20%)
  matrix products  92.7 us (17%)
  starting transfers between devices  57.5 us (11%)
  between operations  47.5 us (9%)
  other arithmetic  25.7 us (5%)
  local copies, waits for them, and re-layouts  24.5 us (4%)
    ppermute x24, waiting for transfers between devices, right(): return lax.ppermute(value, 'cell', forth)  85.6 us
    dot_general x72, matrix products, dot(): lax.dot_general(left, right, (dims, ((), ())), precision=lax.Precision.HI...  75.5 us
    ppermute x24, waiting for transfers between devices, left(): return lax.ppermute(value, 'cell', back)  56.1 us
    psum x1, blocking collectives, per_device(): losses = lax.psum(jnp.stack(loss_list), ('spot', 'cell'))  39.9 us
    all_gather x3, waiting for transfers between devices, per_device(): full = lax.all_gather(expression[micro], 'spot')  37.6 us
    psum x1, blocking collectives, per_device(): lax.psum((jnp.sum(spot_mask * predicted * predicted, axis=1), jnp.sum(spo...  36.5 us
    ppermute x24, starting transfers between devices, left(): return lax.ppermute(value, 'cell', back)  34.5 us
    psum x1, blocking collectives, per_device(): inverse = 1.0 / lax.psum(jnp.sum(raised, axis=1), 'cell')  23.4 us
  transfers between devices with their start and end apart: 54, of which 38 were waited for; matrix products, arithmetic and copies ran while one was open for 22% of the time, Pallas kernels for 0%

profile of v1, /device:TPU:0, one launch (start us, length us, event | category | flops | bytes accessed | tf_op | source)
XLA Modules:
  0.0 539.3 jit_solution(11804367640073248415)
XLA Ops:
  7.2 3.7 fusion.343
  46.9 23.4 %psum.161 = f32[3,512]{1,0:T(4,128)S(1)} all-reduce(f32[3,512]{1,0:T(4,128)S(1)} %get-tuple-element.63), channel_id=1, replica_groups=mesh['spot'=4,'cell'=8] {'cell'}, use_global_device_ids=true, to_apply=%region_2.3 | all-reduce | flops 1536 | bytes 12288 | tf_op jit(solution)/shard_map/psum | solution.py:78
  79.4 5.5 %all-gather.6.cloned.1.call-done = f32[4,512,512]{2,1,0:T(8,128)} async-done(((f32[1,512,512]{2,1,0:T(8,128)}), f32[4,512,512]{2,1,0:T(8,128)}) %all-gather.6.cloned.1.call-update) | async-done | bytes 4194320 | tf_op jit(solution)/shard_map/all_gather | solution.py:83
  89.5 32.1 %all-gather.4.cloned.1.call-done = f32[4,512,512]{2,1,0:T(8,128)} async-done(((f32[1,512,512]{2,1,0:T(8,128)}), f32[4,512,512]{2,1,0:T(8,128)}) %all-gather.4.cloned.1.call-update) | async-done | bytes 4194320 | tf_op jit(solution)/shard_map/all_gather | solution.py:83
  148.5 6.0 %collective-permute-done.21 = f32[512,256]{0,1:T(8,128)S(1)} collective-permute-done((f32[512,256]{0,1:T(8,128)S(1)}, f32[512,256]{0,1:T(8,128)S(1)}, u32[]{:S(2)}, u32[]{:S(2)}) %collective-permute-start.21) | collective-permute-done | bytes 524320 | tf_op jit(solution)/shard_map/ppermute | solution.py:68
  159.7 6.1 %collective-permute-done.13 = f32[512,256]{0,1:T(8,128)S(1)} collective-permute-done((f32[512,256]{0,1:T(8,128)S(1)}, f32[512,256]{0,1:T(8,128)S(1)}, u32[]{:S(2)}, u32[]{:S(2)}) %collective-permute-start.13) | collective-permute-done | bytes 524320 | tf_op jit(solution)/shard_map/ppermute | solution.py:68
  172.0 5.1 collective-permute-done.5
  182.9 5.4 %collective-permute-done.22 = f32[512,256]{0,1:T(8,128)S(1)} collective-permute-done((f32[512,256]{0,1:T(8,128)S(1)}, f32[512,256]{0,1:T(8,128)S(1)}, u32[]{:S(2)}, u32[]{:S(2)}) %collective-permute-start.22) | collective-permute-done | bytes 524320 | tf_op jit(solution)/shard_map/ppermute | solution.py:68
  193.4 6.1 %collective-permute-done.14 = f32[512,256]{0,1:T(8,128)S(1)} collective-permute-done((f32[512,256]{0,1:T(8,128)S(1)}, f32[512,256]{0,1:T(8,128)S(1)}, u32[]{:S(2)}, u32[]{:S(2)}) %collective-permute-start.14) | collective-permute-done | bytes 524320 | tf_op jit(solution)/shard_map/ppermute | solution.py:68
  204.7 6.1 %collective-permute-done.6 = f32[512,256]{0,1:T(8,128)S(1)} collective-permute-done((f32[512,256]{0,1:T(8,128)S(1)}, f32[512,256]{0,1:T(8,128)S(1)}, u32[]{:S(2)}, u32[]{:S(2)}) %collective-permute-start.6) | collective-permute-done | bytes 524320 | tf_op jit(solution)/shard_map/ppermute | solution.py:68
  215.9 6.1 %collective-permute-done.23 = f32[512,256]{0,1:T(8,128)S(1)} collective-permute-done((f32[512,256]{0,1:T(8,128)S(1)}, f32[512,256]{0,1:T(8,128)S(1)}, u32[]{:S(2)}, u32[]{:S(2)}) %collective-permute-start.23) | collective-permute-done | bytes 524320 | tf_op jit(solution)/shard_map/ppermute | solution.py:68
  226.1 7.1 %collective-permute-done.15 = f32[512,256]{0,1:T(8,128)S(1)} collective-permute-done((f32[512,256]{0,1:T(8,128)S(1)}, f32[512,256]{0,1:T(8,128)S(1)}, u32[]{:S(2)}, u32[]{:S(2)}) %collective-permute-start.15) | collective-permute-done | bytes 524320 | tf_op jit(solution)/shard_map/ppermute | solution.py:68
  233.2 3.6 collective-permute-done.11
  238.1 5.0 collective-permute-done.7
  243.1 3.9 collective-permute-done.3
  248.3 10.7 %all-reduce.1 = (f32[4,256]{1,0:T(4,128)S(1)}, f32[4,256]{1,0:T(4,128)S(1)}, f32[4,256]{1,0:T(4,128)S(1)}, f32[4,256]{1,0:T(4,128)S(1)}, f32[4,256]{1,0:T(4,128)...) all-reduce(f32[4,256]{1,0:T(4,128)S(1)} %fusion.75, ...), channel_id=1, replica_groups=mesh['spot'=4,'cell'=8] {'spot'}, use_global_device_ids=true, to_apply=%region_25.26 | all-reduce | flops 9216 | bytes 73728 | tf_op jit(solution)/shard_map/psum | solution.py:105
  262.4 2.8 fusion.74
  270.1 36.5 %all-reduce = (f32[512]{0:T(512)S(1)}, f32[512]{0:T(512)S(1)}, f32[512]{0:T(512)S(1)}, f32[512]{0:T(512)S(1)}, f32[512]{0:T(512)S(1)}, /*index=5*/f32[512]{0:T(5...) all-reduce(f32[512]{0:T(512)S(1)} %get-tuple-element.25, ...), channel_id=1, replica_groups=mesh['spot'=4,'cell'=8] {'cell'}, use_global_device_ids=true, to_apply=%region_30.31 | all-reduce | flops 6144 | bytes 49152 | tf_op jit(solution)/shard_map/psum | solution.py:123
  314.4 8.0 %collective-permute-done.40 = f32[512,256]{0,1:T(8,128)S(1)} collective-permute-done((f32[512,256]{0,1:T(8,128)S(1)}, f32[512,256]{0,1:T(8,128)S(1)}, u32[]{:S(2)}, u32[]{:S(2)}) %collective-permute-start.40) | collective-permute-done | bytes 524320 | tf_op jit(solution)/shard_map/ppermute | solution.py:65
  327.5 8.0 %collective-permute-done.42 = f32[512,256]{0,1:T(8,128)S(1)} collective-permute-done((f32[512,256]{0,1:T(8,128)S(1)}, f32[512,256]{0,1:T(8,128)S(1)}, u32[]{:S(2)}, u32[]{:S(2)}) %collective-permute-start.42) | collective-permute-done | bytes 524320 | tf_op jit(solution)/shard_map/ppermute | solution.py:65
  340.4 4.6 collective-permute-done.44
  350.1 4.1 collective-permute-done.46
  362.4 2.7 broadcast.96.clone.1
  366.5 5.9 %collective-permute-done.32 = f32[512,256]{0,1:T(8,128)S(1)} collective-permute-done((f32[512,256]{0,1:T(8,128)S(1)}, f32[512,256]{0,1:T(8,128)S(1)}, u32[]{:S(2)}, u32[]{:S(2)}) %collective-permute-start.32) | collective-permute-done | bytes 524320 | tf_op jit(solution)/shard_map/ppermute | solution.py:65
  377.4 7.0 %collective-permute-done.34 = f32[512,256]{0,1:T(8,128)S(1)} collective-permute-done((f32[512,256]{0,1:T(8,128)S(1)}, f32[512,256]{0,1:T(8,128)S(1)}, u32[]{:S(2)}, u32[]{:S(2)}) %collective-permute-start.34) | collective-permute-done | bytes 524320 | tf_op jit(solution)/shard_map/ppermute | solution.py:65
  389.3 5.3 collective-permute-done.36
  413.1 8.4 %collective-permute-done.24 = f32[512,256]{0,1:T(8,128)S(1)} collective-permute-done((f32[512,256]{0,1:T(8,128)S(1)}, f32[512,256]{0,1:T(8,128)S(1)}, u32[]{:S(2)}, u32[]{:S(2)}) %collective-permute-start.24) | collective-permute-done | bytes 524320 | tf_op jit(solution)/shard_map/ppermute | solution.py:65
  426.8 6.1 %collective-permute-done.26 = f32[512,256]{0,1:T(8,128)S(1)} collective-permute-done((f32[512,256]{0,1:T(8,128)S(1)}, f32[512,256]{0,1:T(8,128)S(1)}, u32[]{:S(2)}, u32[]{:S(2)}) %collective-permute-start.26) | collective-permute-done | bytes 524320 | tf_op jit(solution)/shard_map/ppermute | solution.py:65
  438.0 4.1 collective-permute-done.28
  458.4 39.9 %psum.180 = f32[3]{0:T(128)} all-reduce(f32[3]{0:T(128)S(1)} %pad_maximum_fusion.11), channel_id=1, replica_groups=mesh['spot'=4,'cell'=8] {'spot','cell'}, use_global_device_ids=true, to_apply=%region_36.37 | all-reduce | flops 3 | bytes 24 | tf_op jit(solution)/shard_map/psum | solution.py:170
  501.0 3.0 copy.82
  528.2 3.8 pad_maximum_fusion.1
  (395 shorter events, 205.7 us)
Async XLA Ops:
  7.2 67.7 %all-gather.8.cloned.1.call-start = ((), (), s32[]{:S(2)}) async-start(), calls=%async_computation.5 | async-start | bytes 5242880 | tf_op jit(solution)/shard_map/all_gather | solution.py:83
  11.0 74.0 %all-gather.6.cloned.1.call-start = ((), (), s32[]{:S(2)}) async-start(), calls=%async_computation.4 | async-start | bytes 5242880 | tf_op jit(solution)/shard_map/all_gather | solution.py:83
  11.8 109.8 %all-gather.4.cloned.1.call-start = ((), (), s32[]{:S(2)}) async-start(), calls=%async_computation.3 | async-start | bytes 5242880 | tf_op jit(solution)/shard_map/all_gather | solution.py:83
  12.5 515.7 %reduce-scatter.8.cloned.1.call-start = ((), (), s32[]{:S(2)}) async-start(), calls=%async_computation.8 | async-start | bytes 5242880 | tf_op jit(solution)/shard_map/reduce_scatter | solution.py:165
  77.4 60.3 %collective-permute-start.20 = (f32[256,256]{0,1:T(8,128)}, f32[256,256]{0,1:T(8,128)}, u32[]{:S(2)}, u32[]{:S(2)}) collective-permute-start(f32[256,256]{0,1:T(8,128)} %get-tuple-element.86), channel_id=1, source_target_pairs={{3,1},{5,3},{7,5},{6,7},{4,6},{2,4},{0,2},{1,0},{11,9},{13,11},{15... | collective-permute-start | bytes 786440 | tf_op jit(solution)/shard_map/ppermute | solution.py:68
  77.4 62.3 %collective-permute-start.16 = (f32[256,256]{0,1:T(8,128)}, f32[256,256]{0,1:T(8,128)}, u32[]{:S(2)}, u32[]{:S(2)}) collective-permute-start(f32[256,256]{0,1:T(8,128)} %get-tuple-element.85), channel_id=1, source_target_pairs={{1,3},{3,5},{5,7},{7,6},{6,4},{4,2},{2,0},{0,1},{9,11},{11,13},{13... | collective-permute-start | bytes 786440 | tf_op jit(solution)/shard_map/ppermute | solution.py:65
  87.4 54.5 %collective-permute-start.12 = (f32[256,256]{0,1:T(8,128)}, f32[256,256]{0,1:T(8,128)}, u32[]{:S(2)}, u32[]{:S(2)}) collective-permute-start(f32[256,256]{0,1:T(8,128)} %get-tuple-element.80), channel_id=1, source_target_pairs={{3,1},{5,3},{7,5},{6,7},{4,6},{2,4},{0,2},{1,0},{11,9},{13,11},{15... | collective-permute-start | bytes 786440 | tf_op jit(solution)/shard_map/ppermute | solution.py:68
  88.9 55.1 %collective-permute-start.8 = (f32[256,256]{0,1:T(8,128)}, f32[256,256]{0,1:T(8,128)S(1)}, u32[]{:S(2)}, u32[]{:S(2)}) collective-permute-start(f32[256,256]{0,1:T(8,128)} %get-tuple-element.79), channel_id=1, source_target_pairs={{1,3},{3,5},{5,7},{7,6},{6,4},{4,2},{2,0},{0,1},{9,11},{11,13},{13... | collective-permute-start | bytes 786440 | tf_op jit(solution)/shard_map/ppermute | solution.py:65
  123.4 21.8 %collective-permute-start.4 = (f32[256,256]{0,1:T(8,128)S(1)}, f32[256,256]{0,1:T(8,128)S(1)}, u32[]{:S(2)}, u32[]{:S(2)}) collective-permute-start(f32[256,256]{0,1:T(8,128)S(1)} %get-tuple-element.74), channel_id=1, source_target_pairs={{3,1},{5,3},{7,5},{6,7},{4,6},{2,4},{0,2},{1,0},{11,9},{13,11},{15... | collective-permute-start | bytes 786440 | tf_op jit(solution)/shard_map/ppermute | solution.py:68
  139.7 14.8 %collective-permute-start.21 = (f32[512,256]{0,1:T(8,128)S(1)}, f32[512,256]{0,1:T(8,128)S(1)}, u32[]{:S(2)}, u32[]{:S(2)}) collective-permute-start(f32[512,256]{0,1:T(8,128)S(1)} %pad_maximum_fusion.8), channel_id=1, source_target_pairs={{3,1},{5,3},{7,5},{6,7},{4,6},{2,4},{0,2},{1,0},{11,9},{13,11},{15... | collective-permute-start | bytes 1572872 | tf_op jit(solution)/shard_map/ppermute | solution.py:68
  141.9 16.2 %collective-permute-start.17 = (f32[512,256]{0,1:T(8,128)S(1)}, f32[512,256]{0,1:T(8,128)S(1)}, u32[]{:S(2)}, u32[]{:S(2)}) collective-permute-start(f32[512,256]{0,1:T(8,128)S(1)} %pad_maximum_fusion.7), channel_id=1, source_target_pairs={{1,3},{3,5},{5,7},{7,6},{6,4},{4,2},{2,0},{0,1},{9,11},{11,13},{13... | collective-permute-start | bytes 1572872 | tf_op jit(solution)/shard_map/ppermute | solution.py:65
  144.0 21.8 %collective-permute-start.13 = (f32[512,256]{0,1:T(8,128)S(1)}, f32[512,256]{0,1:T(8,128)S(1)}, u32[]{:S(2)}, u32[]{:S(2)}) collective-permute-start(f32[512,256]{0,1:T(8,128)S(1)} %pad_maximum_fusion.6), channel_id=1, source_target_pairs={{3,1},{5,3},{7,5},{6,7},{4,6},{2,4},{0,2},{1,0},{11,9},{13,11},{15... | collective-permute-start | bytes 1572872 | tf_op jit(solution)/shard_map/ppermute | solution.py:68
  145.3 24.1 %collective-permute-start.9 = (f32[512,256]{0,1:T(8,128)S(1)}, f32[512,256]{0,1:T(8,128)S(1)}, u32[]{:S(2)}, u32[]{:S(2)}) collective-permute-start(f32[512,256]{0,1:T(8,128)S(1)} %pad_maximum_fusion.5), channel_id=1, source_target_pairs={{1,3},{3,5},{5,7},{7,6},{6,4},{4,2},{2,0},{0,1},{9,11},{11,13},{13... | collective-permute-start | bytes 1572872 | tf_op jit(solution)/shard_map/ppermute | solution.py:65
  146.9 30.1 %collective-permute-start.5 = (f32[512,256]{0,1:T(8,128)S(1)}, f32[512,256]{0,1:T(8,128)S(1)}, u32[]{:S(2)}, u32[]{:S(2)}) collective-permute-start(f32[512,256]{0,1:T(8,128)S(1)} %pad_maximum_fusion.4), channel_id=1, source_target_pairs={{3,1},{5,3},{7,5},{6,7},{4,6},{2,4},{0,2},{1,0},{11,9},{13,11},{15... | collective-permute-start | bytes 1572872 | tf_op jit(solution)/shard_map/ppermute | solution.py:68
  154.6 26.0 %collective-permute-start.1 = (f32[512,256]{0,1:T(8,128)S(1)}, f32[512,256]{0,1:T(8,128)S(1)}, u32[]{:S(2)}, u32[]{:S(2)}) collective-permute-start(f32[512,256]{0,1:T(8,128)S(1)} %pad_maximum_fusion.3), channel_id=1, source_target_pairs={{1,3},{3,5},{5,7},{7,6},{6,4},{4,2},{2,0},{0,1},{9,11},{11,13},{13... | collective-permute-start | bytes 1572872 | tf_op jit(solution)/shard_map/ppermute | solution.py:65
  158.1 30.1 %collective-permute-start.22 = (f32[512,256]{0,1:T(8,128)S(1)}, f32[512,256]{0,1:T(8,128)S(1)}, u32[]{:S(2)}, u32[]{:S(2)}) collective-permute-start(f32[512,256]{0,1:T(8,128)S(1)} %add.777), channel_id=1, source_target_pairs={{3,1},{5,3},{7,5},{6,7},{4,6},{2,4},{0,2},{1,0},{11,9},{13,11},{15... | collective-permute-start | bytes 1572872 | tf_op jit(solution)/shard_map/ppermute | solution.py:68
  165.8 26.0 %collective-permute-start.18 = (f32[512,256]{0,1:T(8,128)S(1)}, f32[512,256]{0,1:T(8,128)S(1)}, u32[]{:S(2)}, u32[]{:S(2)}) collective-permute-start(f32[512,256]{0,1:T(8,128)S(1)} %add.773), channel_id=1, source_target_pairs={{1,3},{3,5},{5,7},{7,6},{6,4},{4,2},{2,0},{0,1},{9,11},{11,13},{13... | collective-permute-start | bytes 1572872 | tf_op jit(solution)/shard_map/ppermute | solution.py:65
  169.4 30.1 %collective-permute-start.14 = (f32[512,256]{0,1:T(8,128)S(1)}, f32[512,256]{0,1:T(8,128)S(1)}, u32[]{:S(2)}, u32[]{:S(2)}) collective-permute-start(f32[512,256]{0,1:T(8,128)S(1)} %add.766), channel_id=1, source_target_pairs={{3,1},{5,3},{7,5},{6,7},{4,6},{2,4},{0,2},{1,0},{11,9},{13,11},{15... | collective-permute-start | bytes 1572872 | tf_op jit(solution)/shard_map/ppermute | solution.py:68
  177.0 26.0 %collective-permute-start.10 = (f32[512,256]{0,1:T(8,128)S(1)}, f32[512,256]{0,1:T(8,128)S(1)}, u32[]{:S(2)}, u32[]{:S(2)}) collective-permute-start(f32[512,256]{0,1:T(8,128)S(1)} %add.762), channel_id=1, source_target_pairs={{1,3},{3,5},{5,7},{7,6},{6,4},{4,2},{2,0},{0,1},{9,11},{11,13},{13... | collective-permute-start | bytes 1572872 | tf_op jit(solution)/shard_map/ppermute | solution.py:65
  180.6 30.1 %collective-permute-start.6 = (f32[512,256]{0,1:T(8,128)S(1)}, f32[512,256]{0,1:T(8,128)S(1)}, u32[]{:S(2)}, u32[]{:S(2)}) collective-permute-start(f32[512,256]{0,1:T(8,128)S(1)} %add.755), channel_id=1, source_target_pairs={{3,1},{5,3},{7,5},{6,7},{4,6},{2,4},{0,2},{1,0},{11,9},{13,11},{15... | collective-permute-start | bytes 1572872 | tf_op jit(solution)/shard_map/ppermute | solution.py:68
  188.3 26.0 %collective-permute-start.2 = (f32[512,256]{0,1:T(8,128)S(1)}, f32[512,256]{0,1:T(8,128)S(1)}, u32[]{:S(2)}, u32[]{:S(2)}) collective-permute-start(f32[512,256]{0,1:T(8,128)S(1)} %add.733), channel_id=1, source_target_pairs={{1,3},{3,5},{5,7},{7,6},{6,4},{4,2},{2,0},{0,1},{9,11},{11,13},{13... | collective-permute-start | bytes 1572872 | tf_op jit(solution)/shard_map/ppermute | solution.py:65
  191.8 30.1 %collective-permute-start.23 = (f32[512,256]{0,1:T(8,128)S(1)}, f32[512,256]{0,1:T(8,128)S(1)}, u32[]{:S(2)}, u32[]{:S(2)}) collective-permute-start(f32[512,256]{0,1:T(8,128)S(1)} %add.778), channel_id=1, source_target_pairs={{3,1},{5,3},{7,5},{6,7},{4,6},{2,4},{0,2},{1,0},{11,9},{13,11},{15... | collective-permute-start | bytes 1572872 | tf_op jit(solution)/shard_map/ppermute | solution.py:68
  199.5 26.0 %collective-permute-start.19 = (f32[512,256]{0,1:T(8,128)S(1)}, f32[512,256]{0,1:T(8,128)S(1)}, u32[]{:S(2)}, u32[]{:S(2)}) collective-permute-start(f32[512,256]{0,1:T(8,128)S(1)} %add.774), channel_id=1, source_target_pairs={{1,3},{3,5},{5,7},{7,6},{6,4},{4,2},{2,0},{0,1},{9,11},{11,13},{13... | collective-permute-start | bytes 1572872 | tf_op jit(solution)/shard_map/ppermute | solution.py:65
  203.1 30.1 %collective-permute-start.15 = (f32[512,256]{0,1:T(8,128)S(1)}, f32[512,256]{0,1:T(8,128)S(1)}, u32[]{:S(2)}, u32[]{:S(2)}) collective-permute-start(f32[512,256]{0,1:T(8,128)S(1)} %add.767), channel_id=1, source_target_pairs={{3,1},{5,3},{7,5},{6,7},{4,6},{2,4},{0,2},{1,0},{11,9},{13,11},{15... | collective-permute-start | bytes 1572872 | tf_op jit(solution)/shard_map/ppermute | solution.py:68
  210.7 26.0 %collective-permute-start.11 = (f32[512,256]{0,1:T(8,128)S(1)}, f32[512,256]{0,1:T(8,128)S(1)}, u32[]{:S(2)}, u32[]{:S(2)}) collective-permute-start(f32[512,256]{0,1:T(8,128)S(1)} %add.763), channel_id=1, source_target_pairs={{1,3},{3,5},{5,7},{7,6},{6,4},{4,2},{2,0},{0,1},{9,11},{11,13},{13... | collective-permute-start | bytes 1572872 | tf_op jit(solution)/shard_map/ppermute | solution.py:65
  214.3 28.8 %collective-permute-start.7 = (f32[512,256]{0,1:T(8,128)S(1)}, f32[512,256]{0,1:T(8,128)S(1)}, u32[]{:S(2)}, u32[]{:S(2)}) collective-permute-start(f32[512,256]{0,1:T(8,128)S(1)} %add.756), channel_id=1, source_target_pairs={{3,1},{5,3},{7,5},{6,7},{4,6},{2,4},{0,2},{1,0},{11,9},{13,11},{15... | collective-permute-start | bytes 1572872 | tf_op jit(solution)/shard_map/ppermute | solution.py:68
  222.0 25.0 %collective-permute-start.3 = (f32[512,256]{0,1:T(8,128)S(1)}, f32[512,256]{0,1:T(8,128)S(1)}, u32[]{:S(2)}, u32[]{:S(2)}) collective-permute-start(f32[512,256]{0,1:T(8,128)S(1)} %add.734), channel_id=1, source_target_pairs={{1,3},{3,5},{5,7},{7,6},{6,4},{4,2},{2,0},{0,1},{9,11},{11,13},{13... | collective-permute-start | bytes 1572872 | tf_op jit(solution)/shard_map/ppermute | solution.py:65
  308.5 14.6 %collective-permute-start.41 = (f32[512,256]{0,1:T(8,128)S(1)}, f32[512,256]{0,1:T(8,128)S(1)}, u32[]{:S(2)}, u32[]{:S(2)}) collective-permute-start(f32[512,256]{0,1:T(8,128)S(1)} %fusion.82), channel_id=1, source_target_pairs={{3,1},{5,3},{7,5},{6,7},{4,6},{2,4},{0,2},{1,0},{11,9},{13,11},{15... | collective-permute-start | bytes 1572872 | tf_op jit(solution)/shard_map/ppermute | solution.py:68
  358.5 169.7 %reduce-scatter.6.cloned.1.call-start = ((), (), s32[]{:S(2)}) async-start(), calls=%async_computation.7 | async-start | bytes 5242880 | tf_op jit(solution)/shard_map/reduce_scatter | solution.py:165
  405.0 123.2 %reduce-scatter.4.cloned.1.call-start = ((), (), s32[]{:S(2)}) async-start(), calls=%async_computation.6 | async-start | bytes 5242880 | tf_op jit(solution)/shard_map/reduce_scatter | solution.py:165
  407.0 14.6 %collective-permute-start.24 = (f32[512,256]{0,1:T(8,128)S(1)}, f32[512,256]{0,1:T(8,128)S(1)}, u32[]{:S(2)}, u32[]{:S(2)}) collective-permute-start(f32[512,256]{0,1:T(8,128)S(1)} %fusion.138), channel_id=1, source_target_pairs={{1,3},{3,5},{5,7},{7,6},{6,4},{4,2},{2,0},{0,1},{9,11},{11,13},{13... | collective-permute-start | bytes 1572872 | tf_op jit(solution)/shard_map/ppermute | solution.py:65
  407.3 14.4 %collective-permute-start.25 = (f32[512,256]{0,1:T(8,128)S(1)}, f32[512,256]{0,1:T(8,128)S(1)}, u32[]{:S(2)}, u32[]{:S(2)}) collective-permute-start(f32[512,256]{0,1:T(8,128)S(1)} %fusion.138), channel_id=1, source_target_pairs={{3,1},{5,3},{7,5},{6,7},{4,6},{2,4},{0,2},{1,0},{11,9},{13,11},{15... | collective-permute-start | bytes 1572872 | tf_op jit(solution)/shard_map/ppermute | solution.py:68
  (93 other events, 858.2 us)
Sparse Core Ops, SparseCore 0:
  11.1 37.1 all-gather.7
  50.4 34.4 all-gather.5
  87.1 34.4 all-gather.3
  358.6 42.5 reduce-scatter.7
  405.1 43.4 reduce-scatter.5
  451.4 44.8 reduce-scatter.3
